TPU v7x, 32 devices: a whole 2x2x4 slice. The times are simulated.
32 devices in a mesh: dp: 8 (over z, y), tensor: 4 (over x, core).
Axes of the slice: x: 2, y: 2, z: 4, core: 2. Of those that a mesh axis runs over, the one named last changes fastest.
Arguments:
- tokens: int32 [16384], P('dp'), may hold values from 0 to 8190
- lengths: int32 [16, 4], P('dp'), may hold values from 1 to 512, 1024 in all within a row
- timesteps: int32 [16], P('dp'), may hold values from 1 to 1000, as said below
- masks: int32 [16384], P('dp'), may hold values from 0 to 1, as said below
- step_count: int32 [1], replicated, may hold values from 2 to 20
- table: float32 [8192, 768], P('tensor', 'dp'), may hold values from -0.4375 to 0.4375
- joint_weight: float32 [768, 2304], P('dp', 'tensor'), may hold values from -0.21875 to 0.21875
- output_weight: float32 [768, 768], P('tensor', 'dp'), may hold values from -1.75 to 1.75
- upward_weight: float32 [768, 3072], P('dp', 'tensor'), may hold values from -0.21875 to 0.21875
- downward_weight: float32 [3072, 768], P('tensor', 'dp'), may hold values from -0.21875 to 0.21875
- gains: float32 [3, 768], P(None, 'dp'), may hold values from 0.5 to 1.5
- momentum_table: float32 [8192, 768], P('tensor', 'dp'), may hold values from -3.8146973e-06 to 3.8146973e-06
- momentum_joint: float32 [768, 2304], P('dp', 'tensor'), may hold values from -3.8146973e-06 to 3.8146973e-06
- momentum_output: float32 [768, 768], P('tensor', 'dp'), may hold values from -3.8146973e-06 to 3.8146973e-06
- momentum_upward: float32 [768, 3072], P('dp', 'tensor'), may hold values from -3.8146973e-06 to 3.8146973e-06
- momentum_downward: float32 [3072, 768], P('tensor', 'dp'), may hold values from -3.8146973e-06 to 3.8146973e-06
- momentum_gains: float32 [3, 768], P(None, 'dp'), may hold values from -1.9073486e-05 to 1.9073486e-05
- variance_table: float32 [8192, 768], P('tensor', 'dp'), may hold values from 2.9919196e-14 to 1.1967678e-13
- variance_joint: float32 [768, 2304], P('dp', 'tensor'), may hold values from 2.9919196e-14 to 1.1967678e-13
- variance_output: float32 [768, 768], P('tensor', 'dp'), may hold values from 2.9919196e-14 to 1.1967678e-13
- variance_upward: float32 [768, 3072], P('dp', 'tensor'), may hold values from 2.9919196e-14 to 1.1967678e-13
- variance_downward: float32 [3072, 768], P('tensor', 'dp'), may hold values from 2.9919196e-14 to 1.1967678e-13
- variance_gains: float32 [3, 768], P(None, 'dp'), may hold values from 7.4797986e-13 to 2.9919194e-12
Outputs:
- loss: float32 [], replicated
- grad_norm: float32 [], replicated
- new_momentum_table: float32 [8192, 768], P('tensor', 'dp')
- new_variance_table: float32 [8192, 768], P('tensor', 'dp')
- new_table: float32 [8192, 768], P('tensor', 'dp')
- new_momentum_joint: float32 [768, 2304], P('dp', 'tensor')
- new_variance_joint: float32 [768, 2304], P('dp', 'tensor')
- new_joint: float32 [768, 2304], P('dp', 'tensor')
- new_momentum_output: float32 [768, 768], P('tensor', 'dp')
- new_variance_output: float32 [768, 768], P('tensor', 'dp')
- new_output: float32 [768, 768], P('tensor', 'dp')
- new_momentum_upward: float32 [768, 3072], P('dp', 'tensor')
- new_variance_upward: float32 [768, 3072], P('dp', 'tensor')
- new_upward: float32 [768, 3072], P('dp', 'tensor')
- new_momentum_downward: float32 [3072, 768], P('tensor', 'dp')
- new_variance_downward: float32 [3072, 768], P('tensor', 'dp')
- new_downward: float32 [3072, 768], P('tensor', 'dp')
- new_momentum_gains: float32 [3, 768], P(None, 'dp')
- new_variance_gains: float32 [3, 768], P(None, 'dp')
- new_gains: float32 [3, 768], P(None, 'dp')
Inputs may be any that keep to these rules, and one draw needn't show every extreme that they name: `timesteps`: a sequence's timestep is drawn uniformly; some sequence has timestep 1 and some has 1000. `masks`: each position of sequence s is masked independently with probability timesteps[s] / 1000.
All inputs are finite; a program needn't handle non-finite values.
Results may differ from a plain program's by a relative error of at most 0.0082.
Values may be sent and summed in bfloat16 or wider, within the bound.
A program may use at most 192 MiB of HBM per device.

v0:
```python
import jax
import jax.numpy as jnp
from jax import lax
from jax.sharding import PartitionSpec as P

D = 768
HEAD_DIM = 64
VOCAB = 8192
SEQ_LEN = 1024
DOCS = 4
T_DIFF = 1000
eps_norm = 1e-06
neg_fill = -1000000000.0
beta_one = 0.9
beta_two = 0.999
adam_eps = 1e-08
clip_at = 0.02
rates = (0.05, 0.03, 0.25, 0.03, 0.03, 0.3)
decays = (0.1, 0.1, 0.1, 0.1, 0.1, 0.0)


def joined(value, axis, join):
    pieces = jax.tree.map(lambda part: lax.all_gather(part, axis), value)
    head = jax.tree.map(lambda part: part[0], pieces)
    tail = jax.tree.map(lambda part: part[1:], pieces)
    running, _ = lax.scan(lambda running, piece: (join(running, piece), None), head, tail)
    return running


def tensor_total(partial_value):
    return lax.psum(partial_value, "tensor")


def norm_apply(values, gain):
    inverse = lax.rsqrt(jnp.mean(values * values, axis=-1, keepdims=True) + eps_norm)
    return values * inverse * gain


def norm_back(values, gain, upstream):
    inverse = lax.rsqrt(jnp.mean(values * values, axis=-1, keepdims=True) + eps_norm)
    gain_grad = jnp.sum(upstream * values * inverse, axis=0)
    scaled = upstream * gain
    inner = jnp.mean(scaled * values, axis=-1, keepdims=True)
    return (inverse * (scaled - values * inverse * inverse * inner), gain_grad)


def rotate(values, cosine, sine):
    middle = values.shape[-1] // 2
    front_part = values[..., :middle]
    back_part = values[..., middle:]
    return jnp.concatenate(
        [front_part * cosine - back_part * sine, back_part * cosine + front_part * sine], axis=-1
    )


def gelu_exact(values):
    return jax.nn.gelu(values, approximate=False)


def packing(lengths, tokens, masks, timesteps):
    seq_count = lengths.shape[0]
    position = jnp.arange(SEQ_LEN, dtype=jnp.int32)
    doc_ends = jnp.cumsum(lengths, axis=1)
    doc_starts = doc_ends - lengths
    segment = jnp.sum((position[None, :, None] >= doc_ends[:, None, :]).astype(jnp.int32), axis=2)
    chosen = segment[:, :, None] == jnp.arange(DOCS, dtype=jnp.int32)[None, None, :]
    offset = position[None, :] - jnp.sum(jnp.where(chosen, doc_starts[:, None, :], 0), axis=2)
    is_real = segment < DOCS - 1
    targets = tokens.reshape(seq_count, SEQ_LEN)
    corrupt = masks.reshape(seq_count, SEQ_LEN) == 1
    inputs = jnp.where(corrupt, VOCAB - 1, targets)
    factor = jnp.where(timesteps == 1, 1.0, T_DIFF / timesteps.astype(jnp.float32))
    weights = jnp.where(corrupt & is_real, factor[:, None], 0.0)
    inverse_freq = 10000.0 ** (-jnp.arange(HEAD_DIM // 2, dtype=jnp.float32) / (HEAD_DIM // 2))
    angles = offset.astype(jnp.float32)[:, :, None] * inverse_freq
    return (inputs, targets, weights, segment, is_real, jnp.cos(angles), jnp.sin(angles))


def scores_of(query, key_rows, segment):
    same_doc = segment[:, None] == segment[None, :]
    scores = jnp.einsum(
        "qhe,khe->hqk", query, key_rows, preferred_element_type=jnp.float32
    ) * HEAD_DIM ** (-0.5)
    return jnp.where(same_doc[None], scores, neg_fill)


def attend_one(query, key_rows, value_rows, segment):
    scores = scores_of(query, key_rows, segment)
    row_max = jnp.max(scores, axis=-1, keepdims=True)
    expd = jnp.exp(scores - row_max)
    summed = jnp.sum(expd, axis=-1, keepdims=True)
    probs = (expd / summed).astype(jnp.bfloat16)
    output = jnp.einsum("hqk,khe->qhe", probs, value_rows, preferred_element_type=jnp.float32)
    return (output.astype(jnp.bfloat16), (row_max + jnp.log(summed))[..., 0])


def attend_back(query, key_rows, value_rows, segment, row_lse, grad_out):
    scores = scores_of(query, key_rows, segment)
    probs = jnp.exp(scores - row_lse[..., None])
    value_grad = jnp.einsum(
        "hqk,qhe->khe", probs.astype(jnp.bfloat16), grad_out, preferred_element_type=jnp.float32
    )
    prob_grad = jnp.einsum("qhe,khe->hqk", grad_out, value_rows, preferred_element_type=jnp.float32)
    inner = jnp.sum(prob_grad * probs, axis=-1, keepdims=True)
    score_grad = (probs * (prob_grad - inner)).astype(jnp.bfloat16)
    query_grad = jnp.einsum(
        "hqk,khe->qhe", score_grad, key_rows, preferred_element_type=jnp.float32
    ) * HEAD_DIM ** (-0.5)
    key_grad = jnp.einsum(
        "hqk,qhe->khe", score_grad, query, preferred_element_type=jnp.float32
    ) * HEAD_DIM ** (-0.5)
    return (query_grad, key_grad, value_grad)


def vocab_stats(normed, vocab_rows, targets, vocab_start):
    logits = jnp.einsum("rd,vd->rv", normed, vocab_rows, preferred_element_type=jnp.float32)
    local_max = jnp.max(logits, axis=-1)
    local_sum = jnp.sum(jnp.exp(logits - local_max[:, None]), axis=-1)
    target_hit = (targets - vocab_start)[:, None] == jnp.arange(
        vocab_rows.shape[0], dtype=jnp.int32
    )[None, :]
    return (local_max, local_sum, jnp.sum(jnp.where(target_hit, logits, 0.0), axis=-1))


def vocab_back(normed, vocab_rows, targets, vocab_start, row_lse, row_weight):
    logits = jnp.einsum("rd,vd->rv", normed, vocab_rows, preferred_element_type=jnp.float32)
    target_hit = (
        (targets - vocab_start)[:, None]
        == jnp.arange(vocab_rows.shape[0], dtype=jnp.int32)[None, :]
    ).astype(jnp.float32)
    logit_grad = (row_weight[:, None] * (jnp.exp(logits - row_lse[:, None]) - target_hit)).astype(
        jnp.bfloat16
    )
    table_part = jnp.einsum("rv,rd->vd", logit_grad, normed, preferred_element_type=jnp.float32)
    normed_grad = jnp.einsum(
        "rv,vd->rd", logit_grad, vocab_rows, preferred_element_type=jnp.float32
    )
    return (table_part, normed_grad)


def combine(earlier, later):
    max_early, sum_early, pick_early = earlier
    max_late, sum_late, pick_late = later
    top_value = jnp.maximum(max_early, max_late)
    return (
        top_value,
        sum_early * jnp.exp(max_early - top_value) + sum_late * jnp.exp(max_late - top_value),
        pick_early + pick_late,
    )


def per_device(
    tokens,
    lengths,
    timesteps,
    masks,
    step_count,
    table,
    joint_weight,
    output_weight,
    upward_weight,
    downward_weight,
    gains,
    momentum_table,
    momentum_joint,
    momentum_output,
    momentum_upward,
    momentum_downward,
    momentum_gains,
    variance_table,
    variance_joint,
    variance_output,
    variance_upward,
    variance_downward,
    variance_gains,
):
    vocab_rows, joint_rows, output_rows, upward_rows, downward_rows, gain_rows = (
        lax.all_gather(table.astype(jnp.bfloat16), "dp", axis=1, tiled=True),
        lax.all_gather(joint_weight.astype(jnp.bfloat16), "dp", axis=0, tiled=True),
        lax.all_gather(output_weight.astype(jnp.bfloat16), "dp", axis=1, tiled=True),
        lax.all_gather(upward_weight.astype(jnp.bfloat16), "dp", axis=0, tiled=True),
        lax.all_gather(downward_weight.astype(jnp.bfloat16), "dp", axis=1, tiled=True),
        lax.all_gather(gains.astype(jnp.bfloat16), "dp", axis=1, tiled=True),
    )
    gain_full = gain_rows.astype(jnp.float32)
    inputs, targets, weights, segment, is_real, cosine, sine = packing(
        lengths, tokens, masks, timesteps
    )
    seq_count = lengths.shape[0]
    row_count = tokens.shape[0]
    vocab_local = vocab_rows.shape[0]
    vocab_start = lax.axis_index("tensor") * vocab_local
    local_ids = inputs.reshape(row_count) - vocab_start
    inside = (local_ids >= 0) & (local_ids < vocab_local)
    safe_ids = jnp.clip(local_ids, 0, vocab_local - 1)
    looked = jnp.take(vocab_rows, safe_ids, axis=0).astype(jnp.float32) * D**0.5
    embedded = tensor_total(jnp.where(inside[:, None], looked, 0.0))
    normed_one = norm_apply(embedded, gain_full[0]).astype(jnp.bfloat16)
    heads_local = joint_rows.shape[1] // (3 * HEAD_DIM)
    projected = jnp.dot(normed_one, joint_rows, preferred_element_type=jnp.float32).reshape(
        seq_count, SEQ_LEN, heads_local, 3, HEAD_DIM
    )
    rot_cos = cosine[:, :, None, :]
    rot_sin = sine[:, :, None, :]
    query = rotate(projected[:, :, :, 0], rot_cos, rot_sin).astype(jnp.bfloat16)
    key_rows = rotate(projected[:, :, :, 1], rot_cos, rot_sin).astype(jnp.bfloat16)
    value_rows = projected[:, :, :, 2].astype(jnp.bfloat16)
    attended, attn_lse = lax.map(
        lambda items: attend_one(*items), (query, key_rows, value_rows, segment)
    )
    attended_flat = attended.reshape(row_count, heads_local * HEAD_DIM)
    attn_part = jnp.dot(attended_flat, output_rows, preferred_element_type=jnp.float32)
    after_attn = embedded + tensor_total(attn_part)
    normed_two = norm_apply(after_attn, gain_full[1]).astype(jnp.bfloat16)
    pre_gelu = jnp.dot(normed_two, upward_rows, preferred_element_type=jnp.float32)
    gelu_value, gelu_pull = jax.vjp(gelu_exact, pre_gelu)
    activated = gelu_value.astype(jnp.bfloat16)
    mlp_part = jnp.dot(activated, downward_rows, preferred_element_type=jnp.float32)
    after_mlp = after_attn + tensor_total(mlp_part)
    normed_out = norm_apply(after_mlp, gain_full[2]).astype(jnp.bfloat16)
    per_seq = normed_out.reshape(seq_count, SEQ_LEN, D)
    stats = lax.map(
        lambda items: vocab_stats(items[0], vocab_rows, items[1], vocab_start), (per_seq, targets)
    )
    row_max, row_sum, row_pick = joined(
        (stats[0].reshape(row_count), stats[1].reshape(row_count), stats[2].reshape(row_count)),
        "tensor",
        combine,
    )
    row_lse = row_max + jnp.log(row_sum)
    loss_local = jnp.sum(weights.reshape(row_count) * (row_lse - row_pick))
    count_local = jnp.sum(is_real.astype(jnp.float32))
    loss_total, count_total = lax.psum((loss_local, count_local), "dp")

    def head_step(carry, items):
        normed_rows, target_rows, lse_rows, weight_rows = items
        table_part, normed_grad = vocab_back(
            normed_rows, vocab_rows, target_rows, vocab_start, lse_rows, weight_rows
        )
        return (carry + table_part, normed_grad)

    table_grad, out_grad = lax.scan(
        head_step,
        jnp.zeros(vocab_rows.shape, jnp.float32),
        (per_seq, targets, row_lse.reshape(seq_count, SEQ_LEN), weights),
    )
    out_grad = tensor_total(out_grad.reshape(row_count, D))
    mlp_grad, gain_three = norm_back(after_mlp, gain_full[2], out_grad)
    mlp_branch = mlp_grad.astype(jnp.bfloat16)
    downward_grad = jnp.einsum(
        "rf,rd->fd", activated, mlp_branch, preferred_element_type=jnp.float32
    )
    act_grad = jnp.einsum(
        "rd,fd->rf", mlp_branch, downward_rows, preferred_element_type=jnp.float32
    )
    up_input = gelu_pull(act_grad)[0].astype(jnp.bfloat16)
    upward_grad = jnp.einsum("rd,rf->df", normed_two, up_input, preferred_element_type=jnp.float32)
    normed_two_grad = tensor_total(
        jnp.einsum("rf,df->rd", up_input, upward_rows, preferred_element_type=jnp.float32)
    )
    attn_in_grad, gain_two = norm_back(after_attn, gain_full[1], normed_two_grad)
    resid_one = mlp_grad + attn_in_grad
    attn_branch = resid_one.astype(jnp.bfloat16)
    output_grad = jnp.einsum(
        "ra,rd->ad", attended_flat, attn_branch, preferred_element_type=jnp.float32
    )
    attended_grad = (
        jnp.einsum("rd,ad->ra", attn_branch, output_rows, preferred_element_type=jnp.float32)
        .astype(jnp.bfloat16)
        .reshape(seq_count, SEQ_LEN, heads_local, HEAD_DIM)
    )
    query_grad, key_grad, value_grad = lax.map(
        lambda items: attend_back(*items),
        (query, key_rows, value_rows, segment, attn_lse, attended_grad),
    )
    query_grad = rotate(query_grad, rot_cos, -rot_sin)
    key_grad = rotate(key_grad, rot_cos, -rot_sin)
    proj_grad = (
        jnp.stack([query_grad, key_grad, value_grad], axis=3)
        .reshape(row_count, heads_local * 3 * HEAD_DIM)
        .astype(jnp.bfloat16)
    )
    joint_grad = jnp.einsum("rd,rc->dc", normed_one, proj_grad, preferred_element_type=jnp.float32)
    normed_one_grad = tensor_total(
        jnp.einsum("rc,dc->rd", proj_grad, joint_rows, preferred_element_type=jnp.float32)
    )
    embed_in, gain_one = norm_back(embedded, gain_full[0], normed_one_grad)
    embed_grad = resid_one + embed_in
    gain_grad = jnp.stack([gain_one, gain_two, gain_three])
    table_grad = table_grad + jax.ops.segment_sum(
        jnp.where(inside[:, None], embed_grad * D**0.5, 0.0), safe_ids, num_segments=vocab_local
    )
    table_sum, joint_sum, output_sum, upward_sum, downward_sum, gain_sum = (
        lax.psum_scatter(table_grad, "dp", scatter_dimension=1, tiled=True),
        lax.psum_scatter(joint_grad, "dp", scatter_dimension=0, tiled=True),
        lax.psum_scatter(output_grad, "dp", scatter_dimension=1, tiled=True),
        lax.psum_scatter(upward_grad, "dp", scatter_dimension=0, tiled=True),
        lax.psum_scatter(downward_grad, "dp", scatter_dimension=1, tiled=True),
        lax.psum_scatter(gain_grad, "dp", scatter_dimension=1, tiled=True),
    )
    reduced = (table_sum, joint_sum, output_sum, upward_sum, downward_sum, gain_sum)
    local_square = jnp.zeros((), jnp.float32)
    for grad_item in reduced[:5]:
        local_square = local_square + jnp.sum(grad_item * grad_item)
    local_square = local_square + jnp.sum(gain_sum * gain_sum) / lax.axis_size("tensor")
    square_total = lax.psum(local_square, ("dp", "tensor"))
    grad_norm = jnp.sqrt(square_total) / count_total
    clip_scale = jnp.minimum(1.0, clip_at / grad_norm)
    loss = loss_total / count_total
    step_float = step_count[0].astype(jnp.float32)
    fix_one = 1.0 - jnp.power(beta_one, step_float)
    fix_two = 1.0 - jnp.power(beta_two, step_float)
    masters = (table, joint_weight, output_weight, upward_weight, downward_weight, gains)
    moments_one = (
        momentum_table,
        momentum_joint,
        momentum_output,
        momentum_upward,
        momentum_downward,
        momentum_gains,
    )
    moments_two = (
        variance_table,
        variance_joint,
        variance_output,
        variance_upward,
        variance_downward,
        variance_gains,
    )
    updated = []
    for index in range(6):
        clipped = reduced[index] / count_total * clip_scale
        moment_one = beta_one * moments_one[index] + (1.0 - beta_one) * clipped
        moment_two = beta_two * moments_two[index] + (1.0 - beta_two) * clipped * clipped
        stepped = moment_one / fix_one / (jnp.sqrt(moment_two / fix_two) + adam_eps)
        master = masters[index]
        updated.extend(
            [moment_one, moment_two, master - rates[index] * (stepped + decays[index] * master)]
        )
    return tuple([loss, grad_norm] + updated)


def solution(mesh):
    placed = (
        P("dp"),
        P("dp", None),
        P("dp"),
        P("dp"),
        P(),
        P("tensor", "dp"),
        P("dp", "tensor"),
        P("tensor", "dp"),
        P("dp", "tensor"),
        P("tensor", "dp"),
        P(None, "dp"),
        P("tensor", "dp"),
        P("dp", "tensor"),
        P("tensor", "dp"),
        P("dp", "tensor"),
        P("tensor", "dp"),
        P(None, "dp"),
        P("tensor", "dp"),
        P("dp", "tensor"),
        P("tensor", "dp"),
        P("dp", "tensor"),
        P("tensor", "dp"),
        P(None, "dp"),
    )
    return jax.shard_map(
        per_device,
        mesh=mesh,
        in_specs=placed,
        out_specs=(
            P(),
            P(),
            P("tensor", "dp"),
            P("tensor", "dp"),
            P("tensor", "dp"),
            P("dp", "tensor"),
            P("dp", "tensor"),
            P("dp", "tensor"),
            P("tensor", "dp"),
            P("tensor", "dp"),
            P("tensor", "dp"),
            P("dp", "tensor"),
            P("dp", "tensor"),
            P("dp", "tensor"),
            P("tensor", "dp"),
            P("tensor", "dp"),
            P("tensor", "dp"),
            P(None, "dp"),
            P(None, "dp"),
            P(None, "dp"),
        ),
        check_vma=False,
    )
```

profile of v0, /device:TPU:0, one launch (start us, length us, event | category | flops | bytes accessed | tf_op | source)
XLA Modules:
  0.0 1683.7 jit_solution(2242139781662490906)
XLA Ops:
  11.9 62.1 %all-gather.8.cloned.1.call-done = bf16[2048,768]{0,1:T(8,128)(2,1)} async-done(((bf16[2048,96]{0,1:T(8,128)(2,1)}), bf16[2048,768]{0,1:T(8,128)(2,1)}) %all-gather.8.cloned.1.call-update) | async-done | bytes 3145744 | tf_op jit(solution)/shard_map/all_gather | solution.py:178
  77.2 9.6 gather_fusion
  91.7 18.2 %all-gather = bf16[8,96,3]{1,2,0:T(4,128)(2,1)S(1)} all-gather(bf16[1,96,3]{1,2,0:T(4,128)(2,1)S(1)} %convert_bitcast_fusion.1), channel_id=1, replica_groups=mesh['dp'=8,'tensor'=4] {'dp'}, dimensions={0}, use_global_device_ids=true | all-gather | bytes 5184 | tf_op jit(solution)/shard_map/all_gather | solution.py:183
  111.0 33.3 %all_gather.30 = bf16[192,768]{0,1:T(8,128)(2,1)} all-gather(bf16[192,96]{0,1:T(8,128)(2,1)S(1)} %copy.126), channel_id=1, replica_groups=mesh['dp'=8,'tensor'=4] {'dp'}, dimensions={1}, use_global_device_ids=true | all-gather | bytes 331776 | tf_op jit(solution)/shard_map/all_gather | solution.py:180
  146.0 32.9 %all_gather.29 = bf16[768,576]{1,0:T(8,128)(2,1)S(1)} all-gather(bf16[96,576]{1,0:T(8,128)(2,1)S(1)} %convert_element_type.106), channel_id=1, replica_groups=mesh['dp'=8,'tensor'=4] {'dp'}, dimensions={0}, use_global_device_ids=true | all-gather | bytes 995328 | tf_op jit(solution)/shard_map/all_gather | solution.py:179
  178.9 30.9 %all-reduce.8.cloned.1.call-done = f32[2048,768]{1,0:T(8,128)} async-done(((f32[2048,768]{1,0:T(8,128)}), f32[2048,768]{1,0:T(8,128)}) %all-reduce.8.cloned.1.call-update) | async-done | bytes 6291472 | tf_op jit(solution)/shard_map/psum | solution.py:31
  218.9 7.5 reshape.255
  236.0 29.3 %while.72 = (s32[]{:T(128)}, bf16[2,1024,3,64]{1,3,2,0:T(8,128)(2,1)}, f32[2,3,1024]{2,1,0:T(4,128)S(1)}, bf16[2,1024,3,64]{1,3,2,0:T(8,128)(2,1)}, s32[2,1024]{...) while((s32[]{:T(128)}, ...), condition=%wide.region_8.9_spmd.clone, body=%wide.region_5.8_spmd.sunk.clone | while | flops 844297216 | bytes 47835256 | solution.py:208
  244.8 5.7 fusion.202
  259.3 5.7 fusion.202
  273.8 118.2 %all-reduce.10.cloned.1.call-done = f32[2048,768]{1,0:T(8,128)} async-done(((f32[2048,768]{1,0:T(8,128)}), f32[2048,768]{1,0:T(8,128)}) %all-reduce.10.cloned.1.call-update) | async-done | bytes 6291472 | tf_op jit(solution)/shard_map/psum | solution.py:31
  392.0 7.9 multiply_reduce_fusion.8
  400.0 36.0 %all-gather.10.cloned.1.call-done = bf16[768,768]{1,0:T(8,128)(2,1)} async-done(((bf16[96,768]{1,0:T(8,128)(2,1)}), bf16[768,768]{1,0:T(8,128)(2,1)}) %all-gather.10.cloned.1.call-update) | async-done | bytes 1179664 | tf_op jit(solution)/shard_map/all_gather | solution.py:181
  435.9 19.1 %multiply_convert_fusion.3 = (bf16[2048,768]{1,0:T(8,128)(2,1)S(1)}, f32[2048,768]{1,0:T(8,128)}, f32[2048,768]{1,0:T(8,128)}) fusion(bf16[768,768]{1,0:T(8,128)(2,1)} %all-gather.10.cloned.1.call-done, f32[2048,768]{1,0:T(8,128)} %get-tuple-element.571, f32[768]{0:T(1024)S(1)} %copy-done.60, f32[2048]{0:T(1024)S(1)} %add_rsqrt_fusion.1), kind=kOutput, calls=%fused_computation.111 | convolution fusion | flops 2522873856 | bytes 23211008 | tf_op jit(solution)/shard_map/dot_general | solution.py:215
  455.1 23.3 %all-gather.12.cloned.1.call-done = bf16[768,768]{0,1:T(8,128)(2,1)} async-done(((bf16[768,96]{0,1:T(8,128)(2,1)}), bf16[768,768]{0,1:T(8,128)(2,1)}) %all-gather.12.cloned.1.call-update) | async-done | bytes 1179664 | tf_op jit(solution)/shard_map/all_gather | solution.py:182
  478.4 5.8 fusion.125
  485.1 117.6 %all-reduce.12.cloned.1.call-done = f32[2048,768]{1,0:T(8,128)} async-done(((f32[2048,768]{1,0:T(8,128)}), f32[2048,768]{1,0:T(8,128)}) %all-reduce.12.cloned.1.call-update) | async-done | bytes 6291472 | tf_op jit(solution)/shard_map/psum | solution.py:31
  602.7 5.4 multiply_reduce_fusion.7
  613.7 16.7 while.73
  630.4 5.2 all-gather.2
  647.4 34.1 %while.76 = (s32[]{:T(128)}, f32[2048,768]{1,0:T(8,128)}, f32[2,1024,768]{2,1,0:T(8,128)}, f32[2,1024]{1,0:T(2,128)S(1)}, bf16[2,1024,768]{2,1,0:T(8,128)(2,1)},...) while((s32[]{:T(128)}, f32[2048,768]{1,0:T(8,128)}, ...), condition=%wide.region_25.26_spmd.clone.clone, body=%wide.region_24.25_spmd.clone.sunk.clone | while | flops 9679406080 | bytes 151032080 | solution.py:242
  647.5 5.7 multiply_convert_fusion.15
  664.5 5.7 multiply_convert_fusion.15
  681.6 119.9 %all-reduce.14.cloned.1.call-done = f32[2048,768]{1,0:T(8,128)} async-done(((f32[2048,768]{1,0:T(8,128)}), f32[2048,768]{1,0:T(8,128)}) %all-reduce.14.cloned.1.call-update) | async-done | bytes 6291472 | tf_op jit(solution)/shard_map/psum | solution.py:31
  801.5 6.3 multiply_reduce_fusion.1
  812.2 8.1 add_convert_fusion
  826.7 119.9 %all-reduce.16.cloned.1.call-done = f32[2048,768]{1,0:T(8,128)} async-done(((f32[2048,768]{1,0:T(8,128)}), f32[2048,768]{1,0:T(8,128)}) %all-reduce.16.cloned.1.call-update) | async-done | bytes 6291472 | tf_op jit(solution)/shard_map/psum | solution.py:31
  946.6 6.1 multiply_reduce_fusion.2
  953.0 5.6 multiply_add_fusion.1
  965.4 50.7 %while.75 = (s32[]{:T(128)}, f32[2,1024,3,64]{1,3,2,0:T(8,128)}, f32[2,1024,3,64]{1,3,2,0:T(8,128)}, bf16[2,1024,3,64]{1,3,2,0:T(8,128)(2,1)}, bf16[2,1024,3,64]...) while((s32[]{:T(128)}, f32[2,1024,3,64]{1,3,2,0:T(8,128)}, ...), condition=%wide.region_32.33_spmd.clone, body=%wide.region_30.32_spmd.sunk.clone | while | flops 2061890560 | bytes 135247168 | solution.py:272
  971.9 7.1 multiply_reduce_fusion.18
  979.1 7.1 multiply_convert_fusion.14
  996.9 7.1 multiply_reduce_fusion.18
  1004.1 7.1 multiply_convert_fusion.14
  1033.1 8.1 fusion.89
  1041.5 8.0 fusion.110
  1049.5 97.3 %all-reduce.18.cloned.1.call-done = f32[2048,768]{1,0:T(8,128)} async-done(((f32[2048,768]{1,0:T(8,128)}), f32[2048,768]{1,0:T(8,128)}) %all-reduce.18.cloned.1.call-update) | async-done | bytes 6291472 | tf_op jit(solution)/shard_map/psum | solution.py:31
  1146.8 5.4 multiply_reduce_fusion.3
  1153.3 7.1 fusion.112
  1160.4 23.7 %scatter_custom_fusion = f32[2048,768]{1,0:T(8,128)} fusion(f32[2048,768]{1,0:T(8,128)} %get-tuple-element.250, s32[2048]{0:T(1024)} %copy-done.65, f32[2048,768]{1,0:T(8,128)} %copy-done.5, f32[2048,768]{1,0:T(8,128)} %all-reduce.18.cloned.1.call-done, f32[2048,768]{1,0:T(8,128)} %all-reduce.8.cloned.1.call-done, f32[2048]{0:T(1024)S(1)} %broadcast_multiply_fusion, ...), kind=kCustom, calls=%fused_computation.95 | custom fusion | flops 15728640 | bytes 25188352 | tf_op jit(solution)/shard_map/scatter-add | solution.py:290
  1184.2 6.6 copy.136
  1192.3 21.7 %all-reduce = (f32[]{:T(128)}, f32[]{:T(128)}) all-reduce(f32[]{:T(128)} %get-tuple-element.564, f32[]{:T(128)} %convert_reduce_fusion.1), channel_id=1, replica_groups=mesh['dp'=8,'tensor'=4] {'dp'}, use_global_device_ids=true, to_apply=%region_21.22 | all-reduce | flops 2 | bytes 16 | tf_op jit(solution)/shard_map/psum | solution.py:233
  1216.4 68.9 %reduce-scatter.17.cloned.1.call-done = f32[768,96]{0,1:T(8,128)} async-done(((f32[768,768]{0,1:T(8,128)}), f32[768,96]{0,1:T(8,128)}) %reduce-scatter.17.cloned.1.call-update) | async-done | bytes 294928 | tf_op jit(solution)/shard_map/reduce_scatter | solution.py:298
  1287.0 70.1 %reduce-scatter.15.cloned.1.call-done = f32[96,768]{1,0:T(8,128)} async-done(((f32[768,768]{1,0:T(8,128)}), f32[96,768]{1,0:T(8,128)}) %reduce-scatter.15.cloned.1.call-update) | async-done | bytes 294928 | tf_op jit(solution)/shard_map/reduce_scatter | solution.py:297
  1358.7 63.0 %reduce-scatter.23.cloned.1.call-done = f32[96,3]{1,0:T(8,128)} async-done(((f32[768,3]{1,0:T(8,128)}), f32[96,3]{1,0:T(8,128)}) %reduce-scatter.23.cloned.1.call-update) | async-done | bytes 1168
  1423.8 67.5 %reduce-scatter.13.cloned.1.call-done = f32[96,576]{1,0:T(8,128)} async-done(((f32[768,576]{1,0:T(8,128)}), f32[96,576]{1,0:T(8,128)}) %reduce-scatter.13.cloned.1.call-update) | async-done | bytes 221200 | tf_op jit(solution)/shard_map/reduce_scatter | solution.py:295
  1492.9 118.5 %reduce-scatter.19.cloned.1.call-done = f32[96,2048]{1,0:T(8,128)} async-done(((f32[768,2048]{1,0:T(8,128)}), f32[96,2048]{1,0:T(8,128)}) %reduce-scatter.19.cloned.1.call-update) | async-done | bytes 786448
  1618.5 39.6 %psum.71 = f32[]{:T(128)} all-reduce(f32[]{:T(128)S(6)} %add.255), channel_id=1, replica_groups=mesh['dp'=8,'tensor'=4] {'dp','tensor'}, use_global_device_ids=true, to_apply=%region_51.52 | all-reduce | flops 1 | bytes 8 | tf_op jit(solution)/shard_map/psum | solution.py:306
  (386 shorter events, 201.1 us)
Async XLA Ops:
  7.2 66.8 %all-gather.8.cloned.1.call-start = ((), (), s32[]{:S(2)}) async-start(), calls=%async_computation.6 | async-start | bytes 3538944 | tf_op jit(solution)/shard_map/all_gather | solution.py:178
  9.2 200.6 %all-reduce.8.cloned.1.call-start = ((), (), s32[]{:S(2)}) async-start(), calls=%async_computation.7 | async-start | bytes 12582912 | tf_op jit(solution)/shard_map/psum | solution.py:31
  10.0 76.8 %copy-start.68 = (pred[2048]{0:T(1024)(128)(4,1)}, pred[2048]{0:T(1024)(128)(4,1)S(1)}, u32[]{:S(2)}) copy-start(pred[2048]{0:T(1024)(128)(4,1)S(1)} %get-tuple-element.572) | copy-start | bytes 6148
  86.8 23.2 %copy-start.45 = (f32[192,96]{1,0:T(8,128)S(1)}, f32[192,96]{1,0:T(8,128)}, u32[]{:S(2)}) copy-start(f32[192,96]{1,0:T(8,128)} %param.40) | copy-start | bytes 221188
  86.8 23.3 %copy-start.36 = (f32[96,576]{1,0:T(8,128)S(1)}, f32[96,576]{1,0:T(8,128)}, u32[]{:S(2)}) copy-start(f32[96,576]{1,0:T(8,128)} %param.39) | copy-start | bytes 663556
  91.4 300.6 %all-reduce.10.cloned.1.call-start = ((), (), s32[]{:S(2)}) async-start(), calls=%async_computation.8 | async-start | bytes 12582912 | tf_op jit(solution)/shard_map/psum | solution.py:31
  110.9 108.1 %copy-start.52 = (f32[768]{0:T(1024)}, f32[768]{0:T(1024)S(1)}, u32[]{:S(2)}) copy-start(f32[768]{0:T(1024)S(1)} %get-tuple-element.457) | copy-start | bytes 9220
  146.0 87.5 %copy-start.25 = (f32[2,1024,32]{1,2,0:T(8,128)}, f32[2,1024,32]{1,2,0:T(8,128)S(1)}, u32[]{:S(2)}) copy-start(f32[2,1024,32]{1,2,0:T(8,128)S(1)} %get-tuple-element.602) | copy-start | bytes 786436
  178.9 40.0 %copy-start.18 = (bf16[768,576]{1,0:T(8,128)(2,1)}, bf16[768,576]{1,0:T(8,128)(2,1)S(1)}, u32[]{:S(2)}) copy-start(bf16[768,576]{1,0:T(8,128)(2,1)S(1)} %all_gather.29) | copy-start | bytes 2654212
  236.0 32.4 %copy-start.20 = (bf16[192,768]{0,1:T(8,128)(2,1)S(1)}, bf16[192,768]{0,1:T(8,128)(2,1)}, u32[]{:S(2)}) copy-start(bf16[192,768]{0,1:T(8,128)(2,1)} %all_gather.30) | copy-start | bytes 884740
  265.3 219.7 %copy-start.43 = (s32[2,1024]{1,0:T(2,128)}, s32[2,1024]{1,0:T(2,128)S(1)}, u32[]{:S(2)}) copy-start(s32[2,1024]{1,0:T(2,128)S(1)} %get-tuple-element.1178) | copy-start | bytes 24580
  272.1 163.9 %all-gather.10.cloned.1.call-start = ((), (), s32[]{:S(2)}) async-start(), calls=%async_computation.9 | async-start | bytes 1327104 | tf_op jit(solution)/shard_map/all_gather | solution.py:181
  272.8 205.6 %all-gather.12.cloned.1.call-start = ((), (), s32[]{:S(2)}) async-start(), calls=%async_computation.10 | async-start | bytes 1327104 | tf_op jit(solution)/shard_map/all_gather | solution.py:182
  273.7 162.2 %copy-start.60 = (f32[768]{0:T(1024)S(1)}, f32[768]{0:T(1024)}, u32[]{:S(2)}) copy-start(f32[768]{0:T(1024)} %get-tuple-element.456) | copy-start | bytes 9220
  273.7 329.0 %all-reduce.12.cloned.1.call-start = ((), (), s32[]{:S(2)}) async-start(), calls=%async_computation.11 | async-start | bytes 12582912 | tf_op jit(solution)/shard_map/psum | solution.py:31
  399.9 55.1 %copy-start.55 = (f32[2048]{0:T(1024)}, f32[2048]{0:T(1024)S(1)}, u32[]{:S(2)}) copy-start(f32[2048]{0:T(1024)S(1)} %add_rsqrt_fusion.1) | copy-start | bytes 24580
  455.1 29.1 %copy-start.81 = (bf16[2048,768]{1,0:T(8,128)(2,1)}, bf16[2048,768]{1,0:T(8,128)(2,1)S(1)}, u32[]{:S(2)}) copy-start(bf16[2048,768]{1,0:T(8,128)(2,1)S(1)} %get-tuple-element.568) | copy-start | bytes 9437188
  484.2 317.2 %all-reduce.14.cloned.1.call-start = ((), (), s32[]{:S(2)}) async-start(), calls=%async_computation.12 | async-start | bytes 12582912 | tf_op jit(solution)/shard_map/psum | solution.py:31
  485.0 123.0 %copy-start.63 = (pred[2,1024]{1,0:T(4,128)(4,1)}, pred[2,1024]{1,0:T(4,128)(4,1)S(1)}, u32[]{:S(2)}) copy-start(pred[2,1024]{1,0:T(4,128)(4,1)S(1)} %get-tuple-element.563) | copy-start | bytes 6148
  485.1 126.2 %copy-start.58 = (f32[768]{0:T(1024)S(1)}, f32[768]{0:T(1024)}, u32[]{:S(2)}) copy-start(f32[768]{0:T(1024)} %get-tuple-element.455) | copy-start | bytes 9220
  681.5 120.0 %copy-start.51 = (f32[2048]{0:T(1024)S(1)}, f32[2048]{0:T(1024)}, u32[]{:S(2)}) copy-start(f32[2048]{0:T(1024)} %copy-done.50) | copy-start | bytes 24580
  681.5 120.0 %copy-start.59 = (f32[768]{0:T(1024)S(1)}, f32[768]{0:T(1024)}, u32[]{:S(2)}) copy-start(f32[768]{0:T(1024)} %get-tuple-element.455) | copy-start | bytes 9220
  681.5 265.1 %all-reduce.16.cloned.1.call-start = ((), (), s32[]{:S(2)}) async-start(), calls=%async_computation.13 | async-start | bytes 12582912 | tf_op jit(solution)/shard_map/psum | solution.py:31
  801.5 10.2 slice-start
  812.2 9.9 copy-start.77
  826.6 120.0 %copy-start.56 = (f32[2048]{0:T(1024)S(1)}, f32[2048]{0:T(1024)}, u32[]{:S(2)}) copy-start(f32[2048]{0:T(1024)} %copy-done.55) | copy-start | bytes 24580
  826.6 120.0 %copy-start.61 = (f32[768]{0:T(1024)S(1)}, f32[768]{0:T(1024)}, u32[]{:S(2)}) copy-start(f32[768]{0:T(1024)} %get-tuple-element.456) | copy-start | bytes 9220
  826.6 320.2 %all-reduce.18.cloned.1.call-start = ((), (), s32[]{:S(2)}) async-start(), calls=%async_computation.14 | async-start | bytes 12582912 | tf_op jit(solution)/shard_map/psum | solution.py:31
  965.4 50.7 %copy-start.26 = (f32[2,1024,32]{1,2,0:T(8,128)S(1)}, f32[2,1024,32]{1,2,0:T(8,128)}, u32[]{:S(2)}) copy-start(f32[2,1024,32]{1,2,0:T(8,128)} %copy-done.25) | copy-start | bytes 786436
  1026.9 187.9 %reduce-scatter.21.cloned.1.call-start = ((), (), s32[]{:S(2)}) async-start(), calls=%async_computation.19 | async-start | bytes 884736
  1033.0 252.2 %reduce-scatter.17.cloned.1.call-start = ((), (), s32[]{:S(2)}) async-start(), calls=%async_computation.17 | async-start | bytes 2654208 | tf_op jit(solution)/shard_map/reduce_scatter | solution.py:298
  1041.2 105.6 %copy-start.47 = (f32[2048]{0:T(1024)S(1)}, f32[2048]{0:T(1024)}, u32[]{:S(2)}) copy-start(f32[2048]{0:T(1024)} %copy-done.46) | copy-start | bytes 24580
  1041.2 105.6 %copy-start.53 = (f32[768]{0:T(1024)S(1)}, f32[768]{0:T(1024)}, u32[]{:S(2)}) copy-start(f32[768]{0:T(1024)} %copy-done.52) | copy-start | bytes 9220
  1041.2 315.8 %reduce-scatter.15.cloned.1.call-start = ((), (), s32[]{:S(2)}) async-start(), calls=%async_computation.16 | async-start | bytes 2654208 | tf_op jit(solution)/shard_map/reduce_scatter | solution.py:297
  1049.4 372.2 %reduce-scatter.23.cloned.1.call-start = ((), (), s32[]{:S(2)}) async-start(), calls=%async_computation.20 | async-start | bytes 442368
  1153.2 338.0 %reduce-scatter.13.cloned.1.call-start = ((), (), s32[]{:S(2)}) async-start(), calls=%async_computation.15 | async-start | bytes 2211840 | tf_op jit(solution)/shard_map/reduce_scatter | solution.py:295
  1160.4 451.0 %reduce-scatter.19.cloned.1.call-start = ((), (), s32[]{:S(2)}) async-start(), calls=%async_computation.18 | async-start | bytes 7077888
  1190.8 468.9 %copy-start.73 = (f32[3,96]{1,0:T(4,128)S(1)}, f32[3,96]{1,0:T(4,128)}, u32[]{:S(2)}) copy-start(f32[3,96]{1,0:T(4,128)} %param.43) | copy-start | bytes 3460
  1190.8 468.9 %copy-start.75 = (f32[3,96]{1,0:T(4,128)S(1)}, f32[3,96]{1,0:T(4,128)}, u32[]{:S(2)}) copy-start(f32[3,96]{1,0:T(4,128)} %param.55) | copy-start | bytes 3460
  1190.8 468.9 %copy-start.76 = (f32[3,96]{1,0:T(4,128)S(1)}, f32[3,96]{1,0:T(4,128)}, u32[]{:S(2)}) copy-start(f32[3,96]{1,0:T(4,128)} %param.49) | copy-start | bytes 3460
  1190.8 475.7 %copy-start.32 = (f32[768,96]{0,1:T(8,128)S(1)}, f32[768,96]{0,1:T(8,128)}, u32[]{:S(2)}) copy-start(f32[768,96]{0,1:T(8,128)} %param.42) | copy-start | bytes 884740
  1190.8 478.5 %copy-start.34 = (f32[96,768]{1,0:T(8,128)S(1)}, f32[96,768]{1,0:T(8,128)}, u32[]{:S(2)}) copy-start(f32[96,768]{1,0:T(8,128)} %param.41) | copy-start | bytes 884740
  1190.8 481.3 %copy-start.24 = (f32[2048,96]{0,1:T(8,128)S(1)}, f32[2048,96]{0,1:T(8,128)}, u32[]{:S(2)}) copy-start(f32[2048,96]{0,1:T(8,128)} %param.38) | copy-start | bytes 2359300
  1215.7 395.7 %copy-start.37 = (f32[192,96]{1,0:T(8,128)}, f32[192,96]{1,0:T(8,128)S(1)}, u32[]{:S(2)}) copy-start(f32[192,96]{1,0:T(8,128)S(1)} %copy.139) | copy-start | bytes 221188
  1285.2 381.3 %copy-start.35 = (f32[768,96]{0,1:T(8,128)S(1)}, f32[768,96]{0,1:T(8,128)}, u32[]{:S(2)}) copy-start(f32[768,96]{0,1:T(8,128)} %reduce-scatter.17.cloned.1.call-done) | copy-start | bytes 884740
  1611.4 60.7 %copy-start.23 = (f32[96,2048]{1,0:T(8,128)S(1)}, f32[96,2048]{1,0:T(8,128)}, u32[]{:S(2)}) copy-start(f32[96,2048]{1,0:T(8,128)} %reduce-scatter.19.cloned.1.call-done) | copy-start | bytes 2359300
  1613.8 58.3 %copy-start.38 = (f32[2048,96]{0,1:T(8,128)S(1)}, f32[2048,96]{0,1:T(8,128)}, u32[]{:S(2)}) copy-start(f32[2048,96]{0,1:T(8,128)} %param.50) | copy-start | bytes 2359300
  1659.6 12.5 copy-start.39
  (63 other events, 266.1 us)
Sparse Core Ops, SparseCore 0:
  10.8 63.1 all-gather.7
  91.6 118.1 all-reduce.7
  272.2 119.7 all-reduce.9
  394.6 41.2 all-gather.9
  438.5 39.8 all-gather.11
  484.3 118.3 all-reduce.11
  681.6 119.7 all-reduce.13
  826.7 119.8 all-reduce.15
  1027.0 119.7 all-reduce.17
  1150.5 62.7 reduce-scatter.20
  1217.2 68.0 reduce-scatter.16
  1289.0 67.9 reduce-scatter.14
  1361.2 60.4 reduce-scatter.22
  1425.4 65.8 reduce-scatter.12
  1494.7 116.6 reduce-scatter.18
where the time goes:
time: 1690 us; the launch traced here: 1680 us
  waiting for transfers between devices  1110 us (66%)
  matrix products  170 us (10%)
  blocking collectives  161 us (10%)
  other arithmetic  141 us (8%)
  local copies, waits for them, and re-layouts  69.4 us (4%)
  between operations  25.8 us (2%)
    psum x6, waiting for transfers between devices, tensor_total(): return lax.psum(partial_value, 'tensor')  604 us
    unnamed x18, waiting for transfers between devices  182 us
    reduce_scatter x1, waiting for transfers between devices, per_device(): lax.psum_scatter(upward_grad, 'dp', scatter_dimension=0, tiled=True)  70.1 us
    reduce_scatter x1, waiting for transfers between devices, per_device(): lax.psum_scatter(downward_grad, 'dp', scatter_dimension=1, tiled=True)  68.9 us
    reduce_scatter x1, waiting for transfers between devices, per_device(): lax.psum_scatter(joint_grad, 'dp', scatter_dimension=0, tiled=True)  67.5 us
    all_gather x1, waiting for transfers between devices, per_device(): lax.all_gather(table.astype(jnp.bfloat16), 'dp', axis=1, tiled=True)  62.1 us
    psum x1, blocking collectives, per_device(): square_total = lax.psum(local_square, ('dp', 'tensor'))  39.6 us
    all_gather x1, waiting for transfers between devices, per_device(): lax.all_gather(upward_weight.astype(jnp.bfloat16), 'dp', axis=0, tiled=True)  36 us
  transfers between devices with their start and end apart: 15, of which 14 were waited for; matrix products, arithmetic and copies ran while one was open for 6% of the time, Pallas kernels for 0%

commit v1 on v0

--- a/solution.py
+++ b/solution.py
@@ -17,6 +17,18 @@
 clip_at = 0.02
 rates = (0.05, 0.03, 0.25, 0.03, 0.03, 0.3)
 decays = (0.1, 0.1, 0.1, 0.1, 0.1, 0.0)
+
+
+def collect(array, axis, dim):
+    ways, here, step = (lax.axis_size(axis), lax.axis_index(axis), array.shape[dim])
+    line, have = (array, 1)
+    while have < ways:
+        line = jnp.concatenate(
+            [line, lax.ppermute(line, axis, [(d, (d - have) % ways) for d in range(ways)])],
+            axis=dim,
+        )
+        have = 2 * have
+    return jnp.roll(line, here * step, axis=dim)
 
 
 def joined(value, axis, join):
@@ -175,7 +187,7 @@
     variance_gains,
 ):
     vocab_rows, joint_rows, output_rows, upward_rows, downward_rows, gain_rows = (
-        lax.all_gather(table.astype(jnp.bfloat16), "dp", axis=1, tiled=True),
+        collect(table.astype(jnp.bfloat16), "dp", 1),
         lax.all_gather(joint_weight.astype(jnp.bfloat16), "dp", axis=0, tiled=True),
         lax.all_gather(output_weight.astype(jnp.bfloat16), "dp", axis=1, tiled=True),
         lax.all_gather(upward_weight.astype(jnp.bfloat16), "dp", axis=0, tiled=True),

time: 1690 us -> 1580 us (0.935)
  waiting for transfers between devices: 1110 us -> 974 us
    ppermute x0 -> x3, waiting for transfers between devices: none -> 96.8 us  [collect(): lax.ppermute(line, axis, [(d, (d - have) % ways) for d in range(ways)])]
    reduce_scatter x1, waiting for transfers between devices: 68.9 us -> 0.01 us  [per_device(): lax.psum_scatter(downward_grad, 'dp', scatter_dimension=1, tiled=True)]
    all_gather x1 -> x0, waiting for transfers between devices: 62.1 us -> none  [per_device(): lax.all_gather(table.astype(jnp.bfloat16), 'dp', axis=1, tiled=True)]
    reduce_scatter x1, waiting for transfers between devices: 70.1 us -> 21.6 us  [per_device(): lax.psum_scatter(upward_grad, 'dp', scatter_dimension=0, tiled=True)]
    all_gather x1, waiting for transfers between devices: 36 us -> 0.03 us  [per_device(): lax.all_gather(upward_weight.astype(jnp.bfloat16), 'dp', axis=0, tiled=True)]
    all_gather x1, waiting for transfers between devices: 23.3 us -> 0.02 us  [per_device(): lax.all_gather(downward_weight.astype(jnp.bfloat16), 'dp', axis=1, tiled=...]
    unnamed x18 -> x17, waiting for transfers between devices: 182 us -> 182 us
  transfers between devices with their start and end apart: 15 -> 17, of which waited for: 14 -> 13; matrix products, arithmetic and copies ran while one was open for 6% -> 7% of each run, Pallas kernels for 0% -> 0%
where the time goes in v1:
time: 1580 us; the launch traced here: 1570 us
  waiting for transfers between devices  974 us (62%)
  matrix products  171 us (11%)
  blocking collectives  165 us (10%)
  other arithmetic  140 us (9%)
  local copies, waits for them, and re-layouts  82.8 us (5%)
  between operations  27.3 us (2%)
    psum x6, waiting for transfers between devices, tensor_total(): return lax.psum(partial_value, 'tensor')  606 us
    unnamed x17, waiting for transfers between devices  182 us
    ppermute x3, waiting for transfers between devices, collect(): lax.ppermute(line, axis, [(d, (d - have) % ways) for d in range(ways)])  96.8 us
    reduce_scatter x1, waiting for transfers between devices, per_device(): lax.psum_scatter(joint_grad, 'dp', scatter_dimension=0, tiled=True)  67.5 us
    psum x1, blocking collectives, per_device(): square_total = lax.psum(local_square, ('dp', 'tensor'))  39.8 us
    all_gather x1, blocking collectives, per_device(): lax.all_gather(output_weight.astype(jnp.bfloat16), 'dp', axis=1, tiled=True)  33.4 us
    all_gather x1, blocking collectives, per_device(): lax.all_gather(joint_weight.astype(jnp.bfloat16), 'dp', axis=0, tiled=True)  32.5 us
  transfers between devices with their start and end apart: 17, of which 13 were waited for; matrix products, arithmetic and copies ran while one was open for 7% of the time, Pallas kernels for 0%

profile of v1, /device:TPU:0, one launch (start us, length us, event | category | flops | bytes accessed | tf_op | source)
XLA Modules:
  0.0 1570.3 jit_solution(7294664880887900606)
XLA Ops:
  9.5 6.1 collective-permute-start
  15.6 11.2 collective-permute-done
  29.3 17.0 %collective-permute-done.1 = bf16[2048,192]{0,1:T(8,128)(2,1)} collective-permute-done((bf16[2048,192]{0,1:T(8,128)(2,1)S(1)}, bf16[2048,192]{0,1:T(8,128)(2,1)}, u32[]{:S(2)}, u32[]{:S(2)}) %collective-permute-start.1) | collective-permute-done | bytes 786464 | tf_op jit(solution)/shard_map/ppermute | solution.py:27
  50.4 68.7 %collective-permute-done.2 = bf16[2048,384]{1,0:T(8,128)(2,1)} collective-permute-done((bf16[2048,384]{1,0:T(8,128)(2,1)}, bf16[2048,384]{1,0:T(8,128)(2,1)}, u32[]{:S(2)}, u32[]{:S(2)}) %collective-permute-start.2) | collective-permute-done | bytes 1572896 | tf_op jit(solution)/shard_map/ppermute | solution.py:27
  119.0 10.9 concatenate.32
  133.5 9.6 gather_fusion
  148.0 21.6 %all-gather = bf16[8,96,3]{1,2,0:T(4,128)(2,1)S(1)} all-gather(bf16[1,96,3]{1,2,0:T(4,128)(2,1)S(1)} %convert_bitcast_fusion.1), channel_id=1, replica_groups=mesh['dp'=8,'tensor'=4] {'dp'}, dimensions={0}, use_global_device_ids=true | all-gather | bytes 5184 | tf_op jit(solution)/shard_map/all_gather | solution.py:195
  170.7 33.4 %all_gather.26 = bf16[192,768]{0,1:T(8,128)(2,1)} all-gather(bf16[192,96]{0,1:T(8,128)(2,1)S(1)} %copy.134), channel_id=1, replica_groups=mesh['dp'=8,'tensor'=4] {'dp'}, dimensions={1}, use_global_device_ids=true | all-gather | bytes 331776 | tf_op jit(solution)/shard_map/all_gather | solution.py:192
  205.8 32.5 %all_gather.25 = bf16[768,576]{1,0:T(8,128)(2,1)S(1)} all-gather(bf16[96,576]{1,0:T(8,128)(2,1)S(1)} %convert_element_type.106), channel_id=1, replica_groups=mesh['dp'=8,'tensor'=4] {'dp'}, dimensions={0}, use_global_device_ids=true | all-gather | bytes 995328 | tf_op jit(solution)/shard_map/all_gather | solution.py:191
  238.3 31.2 %all-reduce.8.cloned.1.call-done = f32[2048,768]{1,0:T(8,128)} async-done(((f32[2048,768]{1,0:T(8,128)}), f32[2048,768]{1,0:T(8,128)}) %all-reduce.8.cloned.1.call-update) | async-done | bytes 6291472 | tf_op jit(solution)/shard_map/psum | solution.py:43
  278.6 7.5 reshape.255
  295.7 29.3 %while.72 = (s32[]{:T(128)}, bf16[2,1024,3,64]{1,3,2,0:T(8,128)(2,1)}, f32[2,3,1024]{2,1,0:T(4,128)S(1)}, bf16[2,1024,3,64]{1,3,2,0:T(8,128)(2,1)}, s32[2,1024]{...) while((s32[]{:T(128)}, ...), condition=%wide.region_8.9_spmd.clone, body=%wide.region_5.8_spmd.sunk.clone | while | flops 844297216 | bytes 47835256 | solution.py:220
  304.5 5.7 fusion.202
  319.0 5.7 fusion.202
  333.5 118.2 %all-reduce.10.cloned.1.call-done = f32[2048,768]{1,0:T(8,128)} async-done(((f32[2048,768]{1,0:T(8,128)}), f32[2048,768]{1,0:T(8,128)}) %all-reduce.10.cloned.1.call-update) | async-done | bytes 6291472 | tf_op jit(solution)/shard_map/psum | solution.py:43
  451.7 7.9 multiply_reduce_fusion.8
  459.7 19.1 %multiply_convert_fusion.3 = (bf16[2048,768]{1,0:T(8,128)(2,1)S(1)}, f32[2048,768]{1,0:T(8,128)}, f32[2048,768]{1,0:T(8,128)}) fusion(bf16[768,768]{1,0:T(8,128)(2,1)} %all-gather.7.cloned.1.call-done, f32[2048,768]{1,0:T(8,128)} %get-tuple-element.520, f32[768]{0:T(1024)S(1)} %copy-done.61, f32[2048]{0:T(1024)S(1)} %add_rsqrt_fusion.1), kind=kOutput, calls=%fused_computation.111 | convolution fusion | flops 2522873856 | bytes 23211008 | tf_op jit(solution)/shard_map/dot_general | solution.py:227
  478.9 6.7 fusion.125
  486.5 119.1 %all-reduce.12.cloned.1.call-done = f32[2048,768]{1,0:T(8,128)} async-done(((f32[2048,768]{1,0:T(8,128)}), f32[2048,768]{1,0:T(8,128)}) %all-reduce.12.cloned.1.call-update) | async-done | bytes 6291472 | tf_op jit(solution)/shard_map/psum | solution.py:43
  605.6 5.4 multiply_reduce_fusion.7
  616.6 16.7 %while.73 = (s32[]{:T(128)}, f32[2,1024]{1,0:T(2,128)S(1)}, f32[2,1024]{1,0:T(2,128)S(1)}, f32[2,1024]{1,0:T(2,128)S(1)}, bf16[2,1024,768]{2,1,0:T(8,128)(2,1)},...) while((s32[]{:T(128)}, f32[2,1024]{1,0:T(2,128)S(1)}, ...), condition=%wide.region_17.18_spmd.clone, body=%wide.region_13.17_spmd.sunk.clone | while | flops 3233806336 | bytes 21549172 | solution.py:234
  650.3 34.0 %while.76 = (s32[]{:T(128)}, f32[2048,768]{1,0:T(8,128)}, f32[2,1024,768]{2,1,0:T(8,128)}, f32[2,1024]{1,0:T(2,128)S(1)}, bf16[2,1024,768]{2,1,0:T(8,128)(2,1)},...) while((s32[]{:T(128)}, f32[2048,768]{1,0:T(8,128)}, ...), condition=%wide.region_25.26_spmd.clone.clone, body=%wide.region_24.25_spmd.clone.sunk.clone | while | flops 9679406080 | bytes 151032080 | solution.py:254
  650.4 5.7 multiply_convert_fusion.15
  667.4 5.6 multiply_convert_fusion.15
  684.4 119.9 %all-reduce.14.cloned.1.call-done = f32[2048,768]{1,0:T(8,128)} async-done(((f32[2048,768]{1,0:T(8,128)}), f32[2048,768]{1,0:T(8,128)}) %all-reduce.14.cloned.1.call-update) | async-done | bytes 6291472 | tf_op jit(solution)/shard_map/psum | solution.py:43
  804.3 6.3 multiply_reduce_fusion.1
  815.0 8.1 add_convert_fusion
  829.6 119.9 %all-reduce.16.cloned.1.call-done = f32[2048,768]{1,0:T(8,128)} async-done(((f32[2048,768]{1,0:T(8,128)}), f32[2048,768]{1,0:T(8,128)}) %all-reduce.16.cloned.1.call-update) | async-done | bytes 6291472 | tf_op jit(solution)/shard_map/psum | solution.py:43
  949.4 6.1 multiply_reduce_fusion.2
  955.9 5.6 multiply_add_fusion.1
  968.2 50.6 %while.75 = (s32[]{:T(128)}, f32[2,1024,3,64]{1,3,2,0:T(8,128)}, f32[2,1024,3,64]{1,3,2,0:T(8,128)}, bf16[2,1024,3,64]{1,3,2,0:T(8,128)(2,1)}, bf16[2,1024,3,64]...) while((s32[]{:T(128)}, f32[2,1024,3,64]{1,3,2,0:T(8,128)}, ...), condition=%wide.region_32.33_spmd.clone, body=%wide.region_30.32_spmd.sunk.clone | while | flops 2061890560 | bytes 135247168 | solution.py:284
  974.7 7.1 multiply_reduce_fusion.18
  981.9 7.1 multiply_convert_fusion.14
  999.7 7.1 multiply_reduce_fusion.18
  1006.9 7.1 multiply_convert_fusion.14
  1035.9 8.1 fusion.89
  1044.2 7.9 fusion.110
  1052.3 97.3 %all-reduce.18.cloned.1.call-done = f32[2048,768]{1,0:T(8,128)} async-done(((f32[2048,768]{1,0:T(8,128)}), f32[2048,768]{1,0:T(8,128)}) %all-reduce.18.cloned.1.call-update) | async-done | bytes 6291472 | tf_op jit(solution)/shard_map/psum | solution.py:43
  1149.6 5.4 multiply_reduce_fusion.3
  1156.1 7.1 fusion.112
  1163.3 23.8 %scatter_custom_fusion = f32[2048,768]{1,0:T(8,128)} fusion(f32[2048,768]{1,0:T(8,128)} %get-tuple-element.250, s32[2048]{0:T(1024)} %copy-done.66, f32[2048,768]{1,0:T(8,128)} %copy-done.5, f32[2048,768]{1,0:T(8,128)} %all-reduce.18.cloned.1.call-done, f32[2048,768]{1,0:T(8,128)} %all-reduce.8.cloned.1.call-done, f32[2048]{0:T(1024)S(1)} %broadcast_multiply_fusion, ...), kind=kCustom, calls=%fused_computation.95 | custom fusion | flops 15728640 | bytes 25188352 | tf_op jit(solution)/shard_map/scatter-add | solution.py:302
  1187.1 6.6 copy.142
  1195.3 21.9 %all-reduce = (f32[]{:T(128)}, f32[]{:T(128)}) all-reduce(f32[]{:T(128)} %get-tuple-element.513, f32[]{:T(128)} %convert_reduce_fusion.1), channel_id=1, replica_groups=mesh['dp'=8,'tensor'=4] {'dp'}, use_global_device_ids=true, to_apply=%region_21.22 | all-reduce | flops 2 | bytes 16 | tf_op jit(solution)/shard_map/psum | solution.py:245
  1221.2 21.6 %reduce-scatter.15.cloned.1.call-done = f32[96,768]{1,0:T(8,128)} async-done(((f32[768,768]{1,0:T(8,128)}), f32[96,768]{1,0:T(8,128)}) %reduce-scatter.15.cloned.1.call-update) | async-done | bytes 294928 | tf_op jit(solution)/shard_map/reduce_scatter | solution.py:309
  1244.5 63.2 %reduce-scatter.23.cloned.1.call-done = f32[96,3]{1,0:T(8,128)} async-done(((f32[768,3]{1,0:T(8,128)}), f32[96,3]{1,0:T(8,128)}) %reduce-scatter.23.cloned.1.call-update) | async-done | bytes 1168
  1309.8 67.5 %reduce-scatter.13.cloned.1.call-done = f32[96,576]{1,0:T(8,128)} async-done(((f32[768,576]{1,0:T(8,128)}), f32[96,576]{1,0:T(8,128)}) %reduce-scatter.13.cloned.1.call-update) | async-done | bytes 221200 | tf_op jit(solution)/shard_map/reduce_scatter | solution.py:307
  1378.9 118.6 %reduce-scatter.19.cloned.1.call-done = f32[96,2048]{1,0:T(8,128)} async-done(((f32[768,2048]{1,0:T(8,128)}), f32[96,2048]{1,0:T(8,128)}) %reduce-scatter.19.cloned.1.call-update) | async-done | bytes 786448
  1504.5 39.8 %psum.71 = f32[]{:T(128)} all-reduce(f32[]{:T(128)S(6)} %add.267), channel_id=1, replica_groups=mesh['dp'=8,'tensor'=4] {'dp','tensor'}, use_global_device_ids=true, to_apply=%region_51.52 | all-reduce | flops 1 | bytes 8 | tf_op jit(solution)/shard_map/psum | solution.py:318
  (398 shorter events, 209.7 us)
Async XLA Ops:
  8.0 42.2 %copy-start.54 = (s32[2048]{0:T(1024)S(1)}, s32[2048]{0:T(1024)}, u32[]{:S(2)}) copy-start(s32[2048]{0:T(1024)} %param.33) | copy-start | bytes 24580
  8.0 42.2 %copy-start.73 = (s32[2048]{0:T(1024)S(1)}, s32[2048]{0:T(1024)}, u32[]{:S(2)}) copy-start(s32[2048]{0:T(1024)} %param.36) | copy-start | bytes 24580
  8.0 261.4 %all-reduce.8.cloned.1.call-start = ((), (), s32[]{:S(2)}) async-start(), calls=%async_computation.6 | async-start | bytes 12582912 | tf_op jit(solution)/shard_map/psum | solution.py:43
  9.5 17.2 %collective-permute-start = (bf16[2048,96]{1,0:T(8,128)(2,1)S(1)}, bf16[2048,96]{1,0:T(8,128)(2,1)S(1)}, u32[]{:S(2)}, u32[]{:S(2)}) collective-permute-start(bf16[2048,96]{1,0:T(8,128)(2,1)S(1)} %copy.124), channel_id=1, source_target_pairs={{0,28},{4,0},{8,4},{12,8},{16,12},{20,16},{24,20},{28,24},{1,29},{... | collective-permute-start | bytes 1179656 | tf_op jit(solution)/shard_map/ppermute | solution.py:27
  27.7 18.6 %collective-permute-start.1 = (bf16[2048,192]{0,1:T(8,128)(2,1)S(1)}, bf16[2048,192]{0,1:T(8,128)(2,1)}, u32[]{:S(2)}, u32[]{:S(2)}) collective-permute-start(bf16[2048,192]{0,1:T(8,128)(2,1)S(1)} %copy.125), channel_id=1, source_target_pairs={{0,24},{4,28},{8,0},{12,4},{16,8},{20,12},{24,16},{28,20},{1,25},{... | collective-permute-start | bytes 2359304 | tf_op jit(solution)/shard_map/ppermute | solution.py:27
  49.8 69.3 %collective-permute-start.2 = (bf16[2048,384]{1,0:T(8,128)(2,1)}, bf16[2048,384]{1,0:T(8,128)(2,1)}, u32[]{:S(2)}, u32[]{:S(2)}) collective-permute-start(bf16[2048,384]{1,0:T(8,128)(2,1)} %pad_maximum_fusion.1), channel_id=1, source_target_pairs={{0,16},{4,20},{8,24},{12,28},{16,0},{20,4},{24,8},{28,12},{1,17},{... | collective-permute-start | bytes 4718600 | tf_op jit(solution)/shard_map/ppermute | solution.py:27
  50.3 68.7 %copy-start.67 = (pred[2048]{0:T(1024)(128)(4,1)}, pred[2048]{0:T(1024)(128)(4,1)S(1)}, u32[]{:S(2)}) copy-start(pred[2048]{0:T(1024)(128)(4,1)S(1)} %get-tuple-element.522) | copy-start | bytes 6148
  50.3 92.7 %copy-start.69 = (pred[2048]{0:T(1024)(128)(4,1)}, pred[2048]{0:T(1024)(128)(4,1)S(1)}, u32[]{:S(2)}) copy-start(pred[2048]{0:T(1024)(128)(4,1)S(1)} %get-tuple-element.521) | copy-start | bytes 6148
  50.3 68.7 %copy-start.66 = (s32[2048]{0:T(1024)}, s32[2048]{0:T(1024)S(1)}, u32[]{:S(2)}) copy-start(s32[2048]{0:T(1024)S(1)} %get-tuple-element.524) | copy-start | bytes 24580
  143.1 26.7 %copy-start.36 = (f32[96,576]{1,0:T(8,128)S(1)}, f32[96,576]{1,0:T(8,128)}, u32[]{:S(2)}) copy-start(f32[96,576]{1,0:T(8,128)} %param.39) | copy-start | bytes 663556
  147.7 304.0 %all-reduce.10.cloned.1.call-start = ((), (), s32[]{:S(2)}) async-start(), calls=%async_computation.7 | async-start | bytes 12582912 | tf_op jit(solution)/shard_map/psum | solution.py:43
  170.6 108.1 %copy-start.52 = (f32[768]{0:T(1024)}, f32[768]{0:T(1024)S(1)}, u32[]{:S(2)}) copy-start(f32[768]{0:T(1024)S(1)} %get-tuple-element.406) | copy-start | bytes 9220
  205.8 87.5 %copy-start.25 = (f32[2,1024,32]{1,2,0:T(8,128)}, f32[2,1024,32]{1,2,0:T(8,128)S(1)}, u32[]{:S(2)}) copy-start(f32[2,1024,32]{1,2,0:T(8,128)S(1)} %get-tuple-element.551) | copy-start | bytes 786436
  238.3 40.3 %copy-start.18 = (bf16[768,576]{1,0:T(8,128)(2,1)}, bf16[768,576]{1,0:T(8,128)(2,1)S(1)}, u32[]{:S(2)}) copy-start(bf16[768,576]{1,0:T(8,128)(2,1)S(1)} %all_gather.25) | copy-start | bytes 2654212
  295.7 32.4 %copy-start.20 = (bf16[192,768]{0,1:T(8,128)(2,1)S(1)}, bf16[192,768]{0,1:T(8,128)(2,1)}, u32[]{:S(2)}) copy-start(bf16[192,768]{0,1:T(8,128)(2,1)} %all_gather.26) | copy-start | bytes 884740
  325.0 161.4 %copy-start.43 = (s32[2,1024]{1,0:T(2,128)}, s32[2,1024]{1,0:T(2,128)S(1)}, u32[]{:S(2)}) copy-start(s32[2,1024]{1,0:T(2,128)S(1)} %get-tuple-element.1126) | copy-start | bytes 24580
  331.8 127.9 %all-gather.7.cloned.1.call-start = ((), (), s32[]{:S(2)}) async-start(), calls=%async_computation.8 | async-start | bytes 1327104 | tf_op jit(solution)/shard_map/all_gather | solution.py:193
  332.5 146.3 %all-gather.9.cloned.1.call-start = ((), (), s32[]{:S(2)}) async-start(), calls=%async_computation.9 | async-start | bytes 1327104 | tf_op jit(solution)/shard_map/all_gather | solution.py:194
  333.4 126.3 %copy-start.61 = (f32[768]{0:T(1024)S(1)}, f32[768]{0:T(1024)}, u32[]{:S(2)}) copy-start(f32[768]{0:T(1024)} %get-tuple-element.405) | copy-start | bytes 9220
  333.4 272.2 %all-reduce.12.cloned.1.call-start = ((), (), s32[]{:S(2)}) async-start(), calls=%async_computation.10 | async-start | bytes 12582912 | tf_op jit(solution)/shard_map/psum | solution.py:43
  485.6 318.7 %all-reduce.14.cloned.1.call-start = ((), (), s32[]{:S(2)}) async-start(), calls=%async_computation.11 | async-start | bytes 12582912 | tf_op jit(solution)/shard_map/psum | solution.py:43
  486.5 124.5 %copy-start.64 = (pred[2,1024]{1,0:T(4,128)(4,1)}, pred[2,1024]{1,0:T(4,128)(4,1)S(1)}, u32[]{:S(2)}) copy-start(pred[2,1024]{1,0:T(4,128)(4,1)S(1)} %get-tuple-element.512) | copy-start | bytes 6148
  486.5 127.7 %copy-start.59 = (f32[768]{0:T(1024)S(1)}, f32[768]{0:T(1024)}, u32[]{:S(2)}) copy-start(f32[768]{0:T(1024)} %get-tuple-element.404) | copy-start | bytes 9220
  684.3 120.0 %copy-start.51 = (f32[2048]{0:T(1024)S(1)}, f32[2048]{0:T(1024)}, u32[]{:S(2)}) copy-start(f32[2048]{0:T(1024)} %copy-done.50) | copy-start | bytes 24580
  684.3 120.0 %copy-start.60 = (f32[768]{0:T(1024)S(1)}, f32[768]{0:T(1024)}, u32[]{:S(2)}) copy-start(f32[768]{0:T(1024)} %get-tuple-element.404) | copy-start | bytes 9220
  684.4 265.1 %all-reduce.16.cloned.1.call-start = ((), (), s32[]{:S(2)}) async-start(), calls=%async_computation.12 | async-start | bytes 12582912 | tf_op jit(solution)/shard_map/psum | solution.py:43
  829.5 120.0 %copy-start.57 = (f32[2048]{0:T(1024)S(1)}, f32[2048]{0:T(1024)}, u32[]{:S(2)}) copy-start(f32[2048]{0:T(1024)} %copy-done.56) | copy-start | bytes 24580
  829.5 120.0 %copy-start.62 = (f32[768]{0:T(1024)S(1)}, f32[768]{0:T(1024)}, u32[]{:S(2)}) copy-start(f32[768]{0:T(1024)} %get-tuple-element.405) | copy-start | bytes 9220
  829.5 320.1 %all-reduce.18.cloned.1.call-start = ((), (), s32[]{:S(2)}) async-start(), calls=%async_computation.13 | async-start | bytes 12582912 | tf_op jit(solution)/shard_map/psum | solution.py:43
  968.2 50.7 %copy-start.26 = (f32[2,1024,32]{1,2,0:T(8,128)S(1)}, f32[2,1024,32]{1,2,0:T(8,128)}, u32[]{:S(2)}) copy-start(f32[2,1024,32]{1,2,0:T(8,128)} %copy-done.25) | copy-start | bytes 786436
  1029.6 188.2 %reduce-scatter.21.cloned.1.call-start = ((), (), s32[]{:S(2)}) async-start(), calls=%async_computation.18 | async-start | bytes 884736
  1035.8 183.7 %reduce-scatter.17.cloned.1.call-start = ((), (), s32[]{:S(2)}) async-start(), calls=%async_computation.16 | async-start | bytes 2654208 | tf_op jit(solution)/shard_map/reduce_scatter | solution.py:310
  1044.0 105.7 %copy-start.47 = (f32[2048]{0:T(1024)S(1)}, f32[2048]{0:T(1024)}, u32[]{:S(2)}) copy-start(f32[2048]{0:T(1024)} %copy-done.46) | copy-start | bytes 24580
  1044.0 105.7 %copy-start.53 = (f32[768]{0:T(1024)S(1)}, f32[768]{0:T(1024)}, u32[]{:S(2)}) copy-start(f32[768]{0:T(1024)} %copy-done.52) | copy-start | bytes 9220
  1044.0 198.8 %reduce-scatter.15.cloned.1.call-start = ((), (), s32[]{:S(2)}) async-start(), calls=%async_computation.15 | async-start | bytes 2654208 | tf_op jit(solution)/shard_map/reduce_scatter | solution.py:309
  1052.2 255.5 %reduce-scatter.23.cloned.1.call-start = ((), (), s32[]{:S(2)}) async-start(), calls=%async_computation.19 | async-start | bytes 442368
  1156.1 221.2 %reduce-scatter.13.cloned.1.call-start = ((), (), s32[]{:S(2)}) async-start(), calls=%async_computation.14 | async-start | bytes 2211840 | tf_op jit(solution)/shard_map/reduce_scatter | solution.py:307
  1163.2 334.3 %reduce-scatter.19.cloned.1.call-start = ((), (), s32[]{:S(2)}) async-start(), calls=%async_computation.17 | async-start | bytes 7077888
  1193.7 352.0 %copy-start.75 = (f32[3,96]{1,0:T(4,128)S(1)}, f32[3,96]{1,0:T(4,128)}, u32[]{:S(2)}) copy-start(f32[3,96]{1,0:T(4,128)} %param.43) | copy-start | bytes 3460
  1193.7 352.0 %copy-start.77 = (f32[3,96]{1,0:T(4,128)S(1)}, f32[3,96]{1,0:T(4,128)}, u32[]{:S(2)}) copy-start(f32[3,96]{1,0:T(4,128)} %param.55) | copy-start | bytes 3460
  1193.7 352.0 %copy-start.78 = (f32[3,96]{1,0:T(4,128)S(1)}, f32[3,96]{1,0:T(4,128)}, u32[]{:S(2)}) copy-start(f32[3,96]{1,0:T(4,128)} %param.49) | copy-start | bytes 3460
  1193.7 358.6 %copy-start.32 = (f32[768,96]{0,1:T(8,128)S(1)}, f32[768,96]{0,1:T(8,128)}, u32[]{:S(2)}) copy-start(f32[768,96]{0,1:T(8,128)} %param.42) | copy-start | bytes 884740
  1193.8 361.4 %copy-start.34 = (f32[96,768]{1,0:T(8,128)S(1)}, f32[96,768]{1,0:T(8,128)}, u32[]{:S(2)}) copy-start(f32[96,768]{1,0:T(8,128)} %param.41) | copy-start | bytes 884740
  1193.8 364.1 %copy-start.24 = (f32[2048,96]{0,1:T(8,128)S(1)}, f32[2048,96]{0,1:T(8,128)}, u32[]{:S(2)}) copy-start(f32[2048,96]{0,1:T(8,128)} %param.38) | copy-start | bytes 2359300
  1218.9 278.6 %copy-start.37 = (f32[192,96]{1,0:T(8,128)}, f32[192,96]{1,0:T(8,128)S(1)}, u32[]{:S(2)}) copy-start(f32[192,96]{1,0:T(8,128)S(1)} %copy.145) | copy-start | bytes 221188
  1219.5 332.9 %copy-start.35 = (f32[768,96]{0,1:T(8,128)S(1)}, f32[768,96]{0,1:T(8,128)}, u32[]{:S(2)}) copy-start(f32[768,96]{0,1:T(8,128)} %reduce-scatter.17.cloned.1.call-done) | copy-start | bytes 884740
  1497.5 60.4 %copy-start.23 = (f32[96,2048]{1,0:T(8,128)S(1)}, f32[96,2048]{1,0:T(8,128)}, u32[]{:S(2)}) copy-start(f32[96,2048]{1,0:T(8,128)} %reduce-scatter.19.cloned.1.call-done) | copy-start | bytes 2359300
  1499.9 58.0 %copy-start.38 = (f32[2048,96]{0,1:T(8,128)S(1)}, f32[2048,96]{0,1:T(8,128)}, u32[]{:S(2)}) copy-start(f32[2048,96]{0,1:T(8,128)} %param.50) | copy-start | bytes 2359300
  (67 other events, 349.7 us)
Sparse Core Ops, SparseCore 0:
  147.9 121.5 all-reduce.7
  331.9 119.7 all-reduce.9
  485.8 119.7 all-reduce.11
  684.5 119.7 all-reduce.13
  829.6 119.7 all-reduce.15
  1029.8 119.8 all-reduce.17
Sparse Core Ops, SparseCore 1:
  335.0 41.6 all-gather.6
  379.3 40.0 all-gather.8
  1035.9 62.9 reduce-scatter.20
  1102.7 68.0 reduce-scatter.16
  1174.7 68.0 reduce-scatter.14
  1247.0 60.6 reduce-scatter.22
  1311.4 65.8 reduce-scatter.12
  1380.7 116.7 reduce-scatter.18
